TPU v7x, 32 devices: a whole 2x2x4 slice. The times are simulated.
32 devices in a mesh: dp: 4 (over y, core), seq: 4 (over z), tensor: 2 (over x).
Axes of the slice: x: 2, y: 2, z: 4, core: 2. Of those that a mesh axis runs over, the one named last changes fastest.
Arguments:
- tokens: bfloat16 [8192, 2048], P(('dp', 'seq')), may hold values from -6 to 6
- out_grad: bfloat16 [8192, 2048], P(('dp', 'seq')), may hold values from -6 to 6
- positions: int32 [4, 2048], P('dp'), may hold values from 0 to 1151, as said below
- attn_gain: float32 [2048], P(('dp', 'seq')), may hold values from 0.5 to 1.5
- q_weight: float32 [2048, 2048], P(('dp', 'seq'), 'tensor'), may hold values from -0.125 to 0.125
- k_weight: float32 [2048, 512], P(('dp', 'seq'), 'tensor'), may hold values from -0.125 to 0.125
- v_weight: float32 [2048, 512], P(('dp', 'seq'), 'tensor'), may hold values from -0.125 to 0.125
- o_weight: float32 [2048, 2048], P(('dp', 'seq'), 'tensor'), may hold values from -1.5 to 1.5
- mlp_gain: float32 [2048], P(('dp', 'seq')), may hold values from 0.5 to 1.5
- gate_weight: float32 [2048, 8192], P(('dp', 'seq'), 'tensor'), may hold values from -0.125 to 0.125
- up_weight: float32 [2048, 8192], P(('dp', 'seq'), 'tensor'), may hold values from -0.125 to 0.125
- down_weight: float32 [2048, 8192], P(('dp', 'seq'), 'tensor'), may hold values from -0.0625 to 0.0625
Outputs:
- output: bfloat16 [8192, 2048], P(('dp', 'seq'))
- tokens_grad: bfloat16 [8192, 2048], P(('dp', 'seq'))
- attn_gain_grad: float32 [2048], P(('dp', 'seq'))
- q_weight_grad: float32 [2048, 2048], P(('dp', 'seq'), 'tensor')
- k_weight_grad: float32 [2048, 512], P(('dp', 'seq'), 'tensor')
- v_weight_grad: float32 [2048, 512], P(('dp', 'seq'), 'tensor')
- o_weight_grad: float32 [2048, 2048], P(('dp', 'seq'), 'tensor')
- mlp_gain_grad: float32 [2048], P(('dp', 'seq'))
- gate_weight_grad: float32 [2048, 8192], P(('dp', 'seq'), 'tensor')
- up_weight_grad: float32 [2048, 8192], P(('dp', 'seq'), 'tensor')
- down_weight_grad: float32 [2048, 8192], P(('dp', 'seq'), 'tensor')
Inputs may be any that keep to these rules, and one draw needn't show every extreme that they name: In each group, every block of 512 rows (aligned) holds 256 prompt tokens followed by 2 whole continuations of 128 rows; the prompt's positions 0 to 1023 each occur once in the group, in a drawn order; a continuation's rows hold positions 1024 to 1151 in order.
All inputs are finite; a program needn't handle non-finite values.
Results may differ from a plain program's by a relative error of at most 0.018.
Values may be sent and summed in bfloat16 or wider, within the bound.
A program may use at most 384 MiB of HBM per device.

v0:
```python
import math
import jax
import jax.numpy as jnp
import numpy as np
from jax import lax
from jax.sharding import PartitionSpec as P

HEAD_DIM = 64
PROMPT = 1024
CONT_LEN = 128
epsilon = 1e-05


def for_sending(array):
    return jax.tree.map(lambda a: a.astype(jnp.bfloat16) if a.dtype == jnp.float32 else a, array)


def rope_freqs(head_width):
    scaled_list = []
    for column in range(head_width // 2):
        inverse = 1.0 / 500000.0 ** (2.0 * column / head_width)
        wavelength = 2.0 * math.pi / inverse
        if wavelength < 2048.0:
            scaled_list.append(inverse)
        elif wavelength > 8192.0:
            scaled_list.append(inverse / 32.0)
        else:
            smooth_mix = (8192.0 / wavelength - 1.0) / 3.0
            scaled_list.append((1.0 - smooth_mix) * inverse / 32.0 + smooth_mix * inverse)
    return np.array(scaled_list, dtype=np.float32)


def rope_apply(values, cos_table, sin_table):
    half_width = values.shape[-1] // 2
    turned = jnp.concatenate([-values[..., half_width:], values[..., :half_width]], axis=-1)
    return values * cos_table + turned * sin_table


def rope_back(grads, cos_table, sin_table):
    half_width = grads.shape[-1] // 2
    twisted = grads * sin_table
    return grads * cos_table + jnp.concatenate(
        [twisted[..., half_width:], -twisted[..., :half_width]], axis=-1
    )


def norm_parts(values):
    inv_rms = lax.rsqrt(jnp.mean(values * values, axis=-1, keepdims=True) + epsilon)
    return (values * inv_rms, inv_rms)


def norm_back(grad_normed, unit_rows, inv_rms, gain_vec):
    grad_unit = grad_normed * gain_vec
    return inv_rms * (
        grad_unit - unit_rows * jnp.mean(grad_unit * unit_rows, axis=-1, keepdims=True)
    )


def times_transposed(left_side, right_side):
    return lax.dot_general(
        left_side, right_side, (((1,), (1,)), ((), ())), preferred_element_type=jnp.float32
    )


def transposed_times(left_side, right_side):
    return lax.dot_general(
        left_side, right_side, (((0,), (0,)), ((), ())), preferred_element_type=jnp.float32
    )


def local(
    tokens,
    out_grad,
    positions,
    attn_gain,
    q_weight,
    k_weight,
    v_weight,
    o_weight,
    mlp_gain,
    gate_weight,
    up_weight,
    down_weight,
):
    seq_count = lax.axis_size("seq")
    seq_rank = lax.axis_index("seq")
    tok_rows = tokens.shape[0]
    prompt_rows = PROMPT // seq_count
    cont_here = (tok_rows - prompt_rows) // CONT_LEN
    all_pos = positions[0]
    own_pos = lax.dynamic_slice_in_dim(all_pos, seq_rank * tok_rows, tok_rows)
    row_offset = jnp.arange(tok_rows, dtype=jnp.int32)
    cont_number = 1 + seq_rank * cont_here + (row_offset - prompt_rows) // CONT_LEN
    own_seg = jnp.where(row_offset < prompt_rows, jnp.zeros_like(row_offset), cont_number)
    prompt_pos = all_pos.reshape(seq_count, tok_rows)[:, :prompt_rows].reshape(-1)
    key_pos = jnp.concatenate([prompt_pos, own_pos[prompt_rows:]])
    key_seg = jnp.concatenate([jnp.zeros_like(prompt_pos), own_seg[prompt_rows:]])
    visible = (key_pos[None, :] <= own_pos[:, None]) & (
        (key_seg[None, :] == 0) | (key_seg[None, :] == own_seg[:, None])
    )
    prompt_count = prompt_pos.shape[0]
    angles = (
        own_pos.astype(jnp.float32)[:, None]
        * jnp.asarray(rope_freqs(HEAD_DIM), jnp.float32)[None, :]
    )
    angles = jnp.concatenate([angles, angles], axis=1)
    cos_table = jnp.cos(angles)[:, None, :]
    sin_table = jnp.sin(angles)[:, None, :]
    score_scale = 1.0 / math.sqrt(HEAD_DIM)

    def attn_pack():
        return (
            attn_gain.astype(jnp.bfloat16),
            q_weight.astype(jnp.bfloat16),
            k_weight.astype(jnp.bfloat16),
            v_weight.astype(jnp.bfloat16),
            o_weight.astype(jnp.bfloat16),
        )

    def mlp_pack():
        return (
            mlp_gain.astype(jnp.bfloat16),
            gate_weight.astype(jnp.bfloat16),
            up_weight.astype(jnp.bfloat16),
            down_weight.astype(jnp.bfloat16),
        )

    attn_set = lax.all_gather(for_sending(attn_pack()), ("dp", "seq"), axis=0, tiled=True)
    mlp_set = lax.all_gather(for_sending(mlp_pack()), ("dp", "seq"), axis=0, tiled=True)
    inputs = tokens.astype(jnp.float32)
    unit_one, rms_one = norm_parts(inputs)
    normed = (unit_one * attn_set[0].astype(jnp.float32)).astype(jnp.bfloat16)
    query_raw = jnp.dot(normed, attn_set[1], preferred_element_type=jnp.float32)
    key_raw = jnp.dot(normed, attn_set[2], preferred_element_type=jnp.float32)
    value_raw = jnp.dot(normed, attn_set[3], preferred_element_type=jnp.float32)
    local_heads = query_raw.shape[1] // HEAD_DIM
    local_kv = key_raw.shape[1] // HEAD_DIM
    group_size = local_heads // local_kv
    queries = rope_apply(
        query_raw.reshape(tok_rows, local_heads, HEAD_DIM), cos_table, sin_table
    ).astype(jnp.bfloat16)
    keys_own = (
        rope_apply(key_raw.reshape(tok_rows, local_kv, HEAD_DIM), cos_table, sin_table)
        .astype(jnp.bfloat16)
        .reshape(tok_rows, -1)
    )
    values_own = value_raw.astype(jnp.bfloat16)
    prompt_keys, prompt_values = (
        lax.all_gather(keys_own[:prompt_rows], "seq", axis=0, tiled=True),
        lax.all_gather(values_own[:prompt_rows], "seq", axis=0, tiled=True),
    )
    key_all = jnp.concatenate([prompt_keys, keys_own[prompt_rows:]], axis=0).reshape(
        -1, local_kv, HEAD_DIM
    )
    value_all = jnp.concatenate([prompt_values, values_own[prompt_rows:]], axis=0).reshape(
        -1, local_kv, HEAD_DIM
    )

    def head_scores(query_group, key_group):
        scores = (
            jnp.einsum("tgd,cd->gtc", query_group, key_group, preferred_element_type=jnp.float32)
            * score_scale
        )
        return jnp.where(visible[None], scores, -1e30)

    mixed_list = []
    log_totals = []
    for kv_head in range(local_kv):
        query_group = queries[:, kv_head * group_size : (kv_head + 1) * group_size, :]
        scores = head_scores(query_group, key_all[:, kv_head, :])
        row_max = jnp.max(scores, axis=-1, keepdims=True)
        exponent = jnp.exp(scores - row_max)
        row_total = jnp.sum(exponent, axis=-1, keepdims=True)
        probability = exponent / row_total
        log_totals.append(row_max + jnp.log(row_total))
        mixed_list.append(
            jnp.einsum(
                "gtc,cd->tgd",
                probability.astype(jnp.bfloat16),
                value_all[:, kv_head, :],
                preferred_element_type=jnp.float32,
            )
        )
    attended = jnp.concatenate(mixed_list, axis=1).reshape(tok_rows, -1).astype(jnp.bfloat16)
    middle = inputs + lax.psum(
        times_transposed(attended, attn_set[4]).astype(jnp.bfloat16), "tensor"
    ).astype(jnp.float32)
    unit_two, rms_two = norm_parts(middle)
    normed_two = (unit_two * mlp_set[0].astype(jnp.float32)).astype(jnp.bfloat16)
    gate_pre = jnp.dot(normed_two, mlp_set[1], preferred_element_type=jnp.float32)
    upward = jnp.dot(normed_two, mlp_set[2], preferred_element_type=jnp.float32)
    sigmoid_gate = jax.nn.sigmoid(gate_pre)
    activated = gate_pre * sigmoid_gate
    hidden = (activated * upward).astype(jnp.bfloat16)
    result = middle + lax.psum(
        times_transposed(hidden, mlp_set[3]).astype(jnp.bfloat16), "tensor"
    ).astype(jnp.float32)
    output = result.astype(jnp.bfloat16)
    grad_out = out_grad.astype(jnp.float32)
    grad_hidden = jnp.dot(out_grad, mlp_set[3], preferred_element_type=jnp.float32)
    grad_gate = (
        grad_hidden * upward * sigmoid_gate * (1.0 + gate_pre * (1.0 - sigmoid_gate))
    ).astype(jnp.bfloat16)
    grad_up = (grad_hidden * activated).astype(jnp.bfloat16)
    grad_normed_two = lax.psum(
        (times_transposed(grad_gate, mlp_set[1]) + times_transposed(grad_up, mlp_set[2])).astype(
            jnp.bfloat16
        ),
        "tensor",
    ).astype(jnp.float32)
    gain_two_grad = jnp.sum(grad_normed_two * unit_two, axis=0)
    grad_middle = grad_out + norm_back(
        grad_normed_two, unit_two, rms_two, mlp_set[0].astype(jnp.float32)
    )

    def summed(term):
        return lax.psum_scatter(
            term.astype(jnp.bfloat16), ("dp", "seq"), scatter_dimension=0, tiled=True
        ).astype(jnp.float32)

    down_grad = summed(transposed_times(out_grad, hidden))
    gate_grad = summed(transposed_times(normed_two, grad_gate))
    up_grad = summed(transposed_times(normed_two, grad_up))
    grad_branch = grad_middle.astype(jnp.bfloat16)
    grad_attended = (
        jnp.dot(grad_branch, attn_set[4], preferred_element_type=jnp.float32)
        .astype(jnp.bfloat16)
        .reshape(tok_rows, local_heads, HEAD_DIM)
    )
    query_grads = []
    key_grads = []
    value_grads = []
    for kv_head in range(local_kv):
        query_group = queries[:, kv_head * group_size : (kv_head + 1) * group_size, :]
        key_group = key_all[:, kv_head, :]
        value_group = value_all[:, kv_head, :]
        grad_group = grad_attended[:, kv_head * group_size : (kv_head + 1) * group_size, :]
        probability = jnp.exp(head_scores(query_group, key_group) - log_totals[kv_head])
        grad_prob = jnp.einsum(
            "tgd,cd->gtc", grad_group, value_group, preferred_element_type=jnp.float32
        )
        row_dot = jnp.sum(probability * grad_prob, axis=-1, keepdims=True)
        grad_scores = (probability * (grad_prob - row_dot)).astype(jnp.bfloat16)
        query_grads.append(
            jnp.einsum("gtc,cd->tgd", grad_scores, key_group, preferred_element_type=jnp.float32)
            * score_scale
        )
        key_grads.append(
            jnp.einsum("gtc,tgd->cd", grad_scores, query_group, preferred_element_type=jnp.float32)
            * score_scale
        )
        value_grads.append(
            jnp.einsum(
                "gtc,tgd->cd",
                probability.astype(jnp.bfloat16),
                grad_group,
                preferred_element_type=jnp.float32,
            )
        )
    grad_queries = jnp.concatenate(query_grads, axis=1)
    grad_keys = jnp.stack(key_grads, axis=1).reshape(-1, local_kv * HEAD_DIM)
    grad_values = jnp.stack(value_grads, axis=1).reshape(-1, local_kv * HEAD_DIM)
    key_share, value_share = (
        lax.psum_scatter(
            grad_keys[:prompt_count].astype(jnp.bfloat16), "seq", scatter_dimension=0, tiled=True
        ).astype(jnp.float32),
        lax.psum_scatter(
            grad_values[:prompt_count].astype(jnp.bfloat16), "seq", scatter_dimension=0, tiled=True
        ).astype(jnp.float32),
    )
    grad_key_own = jnp.concatenate([key_share, grad_keys[prompt_count:]], axis=0).reshape(
        tok_rows, local_kv, HEAD_DIM
    )
    grad_query_raw = (
        rope_back(grad_queries, cos_table, sin_table).reshape(tok_rows, -1).astype(jnp.bfloat16)
    )
    grad_key_raw = (
        rope_back(grad_key_own, cos_table, sin_table).reshape(tok_rows, -1).astype(jnp.bfloat16)
    )
    grad_value_raw = jnp.concatenate([value_share, grad_values[prompt_count:]], axis=0).astype(
        jnp.bfloat16
    )
    grad_normed = lax.psum(
        (
            times_transposed(grad_query_raw, attn_set[1])
            + times_transposed(grad_key_raw, attn_set[2])
            + times_transposed(grad_value_raw, attn_set[3])
        ).astype(jnp.bfloat16),
        "tensor",
    ).astype(jnp.float32)
    gain_one_grad = jnp.sum(grad_normed * unit_one, axis=0)
    grad_inputs = grad_middle + norm_back(
        grad_normed, unit_one, rms_one, attn_set[0].astype(jnp.float32)
    )
    attn_terms = (
        gain_one_grad,
        transposed_times(normed, grad_query_raw),
        transposed_times(normed, grad_key_raw),
        transposed_times(normed, grad_value_raw),
        transposed_times(grad_branch, attended),
        gain_two_grad,
    )
    attn_grads = (
        lax.psum_scatter(attn_terms[0], ("dp", "seq"), scatter_dimension=0, tiled=True),
        summed(attn_terms[1]),
        summed(attn_terms[2]),
        summed(attn_terms[3]),
        summed(attn_terms[4]),
        lax.psum_scatter(attn_terms[5], ("dp", "seq"), scatter_dimension=0, tiled=True),
    )
    return (
        output,
        grad_inputs.astype(jnp.bfloat16),
        attn_grads[0],
        attn_grads[1],
        attn_grads[2],
        attn_grads[3],
        attn_grads[4],
        attn_grads[5],
        gate_grad,
        up_grad,
        down_grad,
    )


def solution(mesh):
    placed = (
        P(("dp", "seq"), None),
        P(("dp", "seq"), None),
        P("dp", None),
        P(("dp", "seq")),
        P(("dp", "seq"), "tensor"),
        P(("dp", "seq"), "tensor"),
        P(("dp", "seq"), "tensor"),
        P(("dp", "seq"), "tensor"),
        P(("dp", "seq")),
        P(("dp", "seq"), "tensor"),
        P(("dp", "seq"), "tensor"),
        P(("dp", "seq"), "tensor"),
    )
    return jax.shard_map(
        local,
        mesh=mesh,
        in_specs=placed,
        out_specs=(
            P(("dp", "seq"), None),
            P(("dp", "seq"), None),
            P(("dp", "seq")),
            P(("dp", "seq"), "tensor"),
            P(("dp", "seq"), "tensor"),
            P(("dp", "seq"), "tensor"),
            P(("dp", "seq"), "tensor"),
            P(("dp", "seq")),
            P(("dp", "seq"), "tensor"),
            P(("dp", "seq"), "tensor"),
            P(("dp", "seq"), "tensor"),
        ),
        check_vma=False,
    )
```

profile of v0, /device:TPU:0, one launch (start us, length us, event | category | flops | bytes accessed | tf_op | source)
XLA Modules:
  0.0 1811.2 jit_solution(7538030029307712680)
XLA Ops:
  18.5 33.9 %all-gather = bf16[16,1,128]{2,1,0:T(2,128)(2,1)S(1)} all-gather(bf16[1,1,128]{2,1,0:T(2,128)(2,1)S(1)} %convert_bitcast_fusion.2), channel_id=1, replica_groups=mesh['dp'=4,'seq'=4,'tensor'=2] {'dp','seq'}, dimensions={0}, use_global_device_ids=true | all-gather | bytes 4352 | tf_op jit(solution)/shard_map/all_gather | solution.py:128
  57.3 15.7 all_gather.35
  76.1 15.8 all-gather.12.cloned.1.call-done
  94.3 19.1 %all_gather.37 = bf16[1024,256]{0,1:T(8,128)(2,1)S(1)} all-gather(bf16[256,256]{0,1:T(8,128)(2,1)S(1)} %bitcast.279), channel_id=1, replica_groups=mesh['dp'=4,'seq'=4,'tensor'=2] {'seq'}, dimensions={0}, use_global_device_ids=true | all-gather | bytes 655360 | tf_op jit(solution)/shard_map/all_gather | solution.py:149
  114.1 31.9 %all-gather.14.cloned.1.call-done = bf16[2048,1024]{1,0:T(8,128)(2,1)} async-done(((bf16[128,1024]{1,0:T(8,128)(2,1)}), bf16[2048,1024]{1,0:T(8,128)(2,1)}) %all-gather.14.cloned.1.call-update) | async-done | bytes 4194320 | tf_op jit(solution)/shard_map/all_gather | solution.py:128
  212.9 31.2 %all-gather.1 = bf16[16,1,128]{2,1,0:T(2,128)(2,1)S(1)} all-gather(bf16[1,1,128]{2,1,0:T(2,128)(2,1)S(1)} %convert_bitcast_fusion.1), channel_id=1, replica_groups=mesh['dp'=4,'seq'=4,'tensor'=2] {'dp','seq'}, dimensions={0}, use_global_device_ids=true | all-gather | bytes 4352 | tf_op jit(solution)/shard_map/all_gather | solution.py:129
  246.6 20.1 %all-reduce.9.cloned.1.call-done = bf16[512,2048]{1,0:T(8,128)(2,1)} async-done(((bf16[512,2048]{1,0:T(8,128)(2,1)}), bf16[512,2048]{1,0:T(8,128)(2,1)}) %all-reduce.9.cloned.1.call-update) | async-done | bytes 2097168 | tf_op jit(solution)/shard_map/psum | solution.py:185
  271.6 124.2 %all-gather.20.cloned.1.call-done = bf16[2048,4096]{1,0:T(8,128)(2,1)} async-done(((bf16[128,4096]{1,0:T(8,128)(2,1)}), bf16[2048,4096]{1,0:T(8,128)(2,1)}) %all-gather.20.cloned.1.call-update) | async-done | bytes 16777232 | tf_op jit(solution)/shard_map/all_gather | solution.py:129
  395.8 15.2 fusion.159
  411.0 112.2 %all-gather.18.cloned.1.call-done = bf16[2048,4096]{1,0:T(8,128)(2,1)} async-done(((bf16[128,4096]{1,0:T(8,128)(2,1)}), bf16[2048,4096]{1,0:T(8,128)(2,1)}) %all-gather.18.cloned.1.call-update) | async-done | bytes 16777232 | tf_op jit(solution)/shard_map/all_gather | solution.py:129
  523.2 15.1 fusion.158
  538.3 112.4 %all-gather.22.cloned.1.call-done = bf16[2048,4096]{1,0:T(8,128)(2,1)} async-done(((bf16[128,4096]{1,0:T(8,128)(2,1)}), bf16[2048,4096]{1,0:T(8,128)(2,1)}) %all-gather.22.cloned.1.call-update) | async-done | bytes 16777232 | tf_op jit(solution)/shard_map/all_gather | solution.py:129
  650.6 22.2 %multiply_convert_fusion = (bf16[512,4096]{1,0:T(8,128)(2,1)}, bf16[512,4096]{1,0:T(8,128)(2,1)}, bf16[512,4096]{1,0:T(8,128)(2,1)}) fusion(f32[512,4096]{1,0:T(8,128)} %fusion.158, f32[512,4096]{1,0:T(8,128)} %fusion.159, bf16[512,2048]{1,0:T(8,128)(2,1)} %param.14, bf16[2048,4096]{1,0:T(8,128)(2,1)} %all-gather.22.cloned.1.call-done), kind=kOutput, calls=%fused_computation.43 | convolution fusion | flops 8621391872 | bytes 48234496 | tf_op jit(solution)/shard_map/dot_general | solution.py:200
  672.8 15.4 fusion.160
  702.5 15.7 convolution_convert_fusion.5
  718.3 45.5 %all-reduce.11.cloned.1.call-done = bf16[512,2048]{1,0:T(8,128)(2,1)} async-done(((bf16[512,2048]{1,0:T(8,128)(2,1)}), bf16[512,2048]{1,0:T(8,128)(2,1)}) %all-reduce.11.cloned.1.call-update) | async-done | bytes 2097168 | tf_op jit(solution)/shard_map/psum | solution.py:205
  923.8 21.0 %copy.109 = bf16[2048,4096]{1,0:T(8,128)(2,1)} copy(bf16[2048,4096]{0,1:T(8,128)(2,1)} %convert_bitcast_fusion) | data formatting | bytes 33554432
  978.6 19.4 %reduce-scatter.18.cloned.1.call-done = bf16[128,256]{1,0:T(8,128)(2,1)} async-done(((bf16[2048,256]{1,0:T(8,128)(2,1)}), bf16[128,256]{1,0:T(8,128)(2,1)}) %reduce-scatter.18.cloned.1.call-update) | async-done | bytes 65552 | tf_op jit(solution)/shard_map/reduce_scatter | solution.py:217
  999.5 108.4 %all-reduce.13.cloned.1.call-done = (bf16[512,2048]{1,0:T(8,128)(2,1)}, bf16[512,2048]{1,0:T(8,128)(2,1)}) async-done(((bf16[512,2048]{1,0:T(8,128)(2,1)}, bf16[512,2048]{1,0:T(8,128)(2,1)}), (bf16[512,2048]{1,0:T(8,128)(2,1)}, bf16[512,2048]{1,0:T(8,128)(2,1)})) %all-reduce.13.cloned.1.call-update) | async-done | bytes 4194320 | tf_op jit(solution)/shard_map/psum | solution.py:195
  1110.8 62.4 %all-reduce.3 = (f32[2048]{0:T(1024)S(1)}, f32[2048]{0:T(1024)S(1)}) all-reduce(f32[2048]{0:T(1024)S(1)} %get-tuple-element.46, f32[2048]{0:T(1024)S(1)} %copy-done.54), channel_id=4, replica_groups=mesh['dp'=4,'seq'=4,'tensor'=2] {'dp','seq'}, use_global_device_ids=true, to_apply=%region_23.24.clone | all-reduce | flops 4096 | bytes 32768
  1186.4 73.8 %reduce-scatter.16.cloned.1.call-done = bf16[128,1024]{1,0:T(8,128)(2,1)} async-done(((bf16[2048,1024]{1,0:T(8,128)(2,1)}), bf16[128,1024]{1,0:T(8,128)(2,1)}) %reduce-scatter.16.cloned.1.call-update) | async-done | bytes 262160 | tf_op jit(solution)/shard_map/reduce_scatter | solution.py:217
  1262.0 178.6 %reduce-scatter.28.cloned.1.call-done = bf16[128,4096]{1,0:T(8,128)(2,1)} async-done(((bf16[2048,4096]{1,0:T(8,128)(2,1)}), bf16[128,4096]{1,0:T(8,128)(2,1)}) %reduce-scatter.28.cloned.1.call-update) | async-done | bytes 1048592
  1443.9 177.2 %reduce-scatter.26.cloned.1.call-done = bf16[128,4096]{1,0:T(8,128)(2,1)} async-done(((bf16[2048,4096]{1,0:T(8,128)(2,1)}), bf16[128,4096]{1,0:T(8,128)(2,1)}) %reduce-scatter.26.cloned.1.call-update) | async-done | bytes 1048592 | tf_op jit(solution)/shard_map/reduce_scatter | solution.py:217
  1623.8 177.8 %reduce-scatter.24.cloned.1.call-done = bf16[128,4096]{1,0:T(8,128)(2,1)} async-done(((bf16[2048,4096]{1,0:T(8,128)(2,1)}), bf16[128,4096]{1,0:T(8,128)(2,1)}) %reduce-scatter.24.cloned.1.call-update) | async-done | bytes 1048592 | tf_op jit(solution)/shard_map/reduce_scatter | solution.py:217
  (341 shorter events, 330.8 us)
Async XLA Ops:
  7.2 48.1 %all-gather.10.cloned.1.call-start = ((), (), s32[]{:S(2)}) async-start(), calls=%async_computation.9 | async-start | bytes 1114112 | tf_op jit(solution)/shard_map/all_gather | solution.py:128
  9.0 82.9 %all-gather.12.cloned.1.call-start = ((), (), s32[]{:S(2)}) async-start(), calls=%async_computation.10 | async-start | bytes 1114112 | tf_op jit(solution)/shard_map/all_gather | solution.py:128
  10.6 135.3 %all-gather.14.cloned.1.call-start = ((), (), s32[]{:S(2)}) async-start(), calls=%async_computation.11 | async-start | bytes 4456448 | tf_op jit(solution)/shard_map/all_gather | solution.py:128
  12.4 185.8 %all-gather.16.cloned.1.call-start = ((), (), s32[]{:S(2)}) async-start(), calls=%async_computation.12 | async-start | bytes 4456448 | tf_op jit(solution)/shard_map/all_gather | solution.py:128
  14.3 252.4 %all-reduce.9.cloned.1.call-start = ((), (), s32[]{:S(2)}) async-start(), calls=%async_computation.13 | async-start | bytes 4194304 | tf_op jit(solution)/shard_map/psum | solution.py:185
  18.5 127.4 %copy-start.55 = (f32[512]{0:T(512)}, f32[512]{0:T(512)S(1)}, u32[]{:S(2)}) copy-start(f32[512]{0:T(512)S(1)} %add_rsqrt_fusion.1) | copy-start | bytes 6148
  52.4 93.5 %copy-start.52 = (f32[16,1,128]{2,1,0:T(1,128)}, f32[16,1,128]{2,1,0:T(1,128)S(1)}, u32[]{:S(2)}) copy-start(f32[16,1,128]{2,1,0:T(1,128)S(1)} %convert_element_type.283) | copy-start | bytes 24580
  54.0 96.8 %copy-start.16 = (f32[512,64]{0,1:T(8,128)}, f32[512,64]{0,1:T(8,128)S(1)}, u32[]{:S(2)}) copy-start(f32[512,64]{0,1:T(8,128)S(1)} %get-tuple-element.70) | copy-start | bytes 393220
  94.3 73.3 %copy-start.10 = (bf16[256,4,64]{0,2,1:T(8,128)(2,1)}, bf16[256,4,64]{0,2,1:T(8,128)(2,1)S(1)}, u32[]{:S(2)}) copy-start(bf16[256,4,64]{0,2,1:T(8,128)(2,1)S(1)} %get-tuple-element.68) | copy-start | bytes 393220
  204.5 191.3 %all-gather.20.cloned.1.call-start = ((), (), s32[]{:S(2)}) async-start(), calls=%async_computation.15 | async-start | bytes 17825792 | tf_op jit(solution)/shard_map/all_gather | solution.py:129
  207.3 315.9 %all-gather.18.cloned.1.call-start = ((), (), s32[]{:S(2)}) async-start(), calls=%async_computation.14 | async-start | bytes 17825792 | tf_op jit(solution)/shard_map/all_gather | solution.py:129
  210.1 440.6 %all-gather.22.cloned.1.call-start = ((), (), s32[]{:S(2)}) async-start(), calls=%async_computation.16 | async-start | bytes 17825792 | tf_op jit(solution)/shard_map/all_gather | solution.py:129
  212.8 550.9 %all-reduce.11.cloned.1.call-start = ((), (), s32[]{:S(2)}) async-start(), calls=%async_computation.17 | async-start | bytes 4194304 | tf_op jit(solution)/shard_map/psum | solution.py:205
  702.5 162.0 %reduce-scatter.14.cloned.1.call-start = ((), (), s32[]{:S(2)}) async-start(), calls=%async_computation.19 | async-start | bytes 655360 | tf_op jit(solution)/shard_map/reduce_scatter | solution.py:267
  811.7 65.9 %reduce-scatter.12.cloned.1.call-start = ((), (), s32[]{:S(2)}) async-start(), calls=%async_computation.18 | async-start | bytes 655360 | tf_op jit(solution)/shard_map/reduce_scatter | solution.py:264
  855.7 121.4 %reduce-scatter.20.cloned.1.call-start = ((), (), s32[]{:S(2)}) async-start(), calls=%async_computation.22 | async-start | bytes 1114112 | tf_op jit(solution)/shard_map/reduce_scatter | solution.py:217
  867.5 130.4 %reduce-scatter.18.cloned.1.call-start = ((), (), s32[]{:S(2)}) async-start(), calls=%async_computation.21 | async-start | bytes 1114112 | tf_op jit(solution)/shard_map/reduce_scatter | solution.py:217
  883.4 224.5 %all-reduce.13.cloned.1.call-start = ((), (), s32[]{:S(2)}) async-start(), calls=%async_computation.27 | async-start | bytes 8388608 | tf_op jit(solution)/shard_map/psum | solution.py:195
  892.9 291.8 %reduce-scatter.22.cloned.1.call-start = ((), (), s32[]{:S(2)}) async-start(), calls=%async_computation.23 | async-start | bytes 4456448 | tf_op jit(solution)/shard_map/reduce_scatter | solution.py:217
  902.9 357.3 %reduce-scatter.16.cloned.1.call-start = ((), (), s32[]{:S(2)}) async-start(), calls=%async_computation.20 | async-start | bytes 4456448 | tf_op jit(solution)/shard_map/reduce_scatter | solution.py:217
  908.8 531.9 %reduce-scatter.28.cloned.1.call-start = ((), (), s32[]{:S(2)}) async-start(), calls=%async_computation.26 | async-start | bytes 17825792
  944.8 676.3 %reduce-scatter.26.cloned.1.call-start = ((), (), s32[]{:S(2)}) async-start(), calls=%async_computation.25 | async-start | bytes 17825792 | tf_op jit(solution)/shard_map/reduce_scatter | solution.py:217
  959.9 841.8 %reduce-scatter.24.cloned.1.call-start = ((), (), s32[]{:S(2)}) async-start(), calls=%async_computation.24 | async-start | bytes 17825792 | tf_op jit(solution)/shard_map/reduce_scatter | solution.py:217
  975.2 135.6 %copy-start.54 = (f32[2048]{0:T(1024)S(1)}, f32[2048]{0:T(1024)}, u32[]{:S(2)}) copy-start(f32[2048]{0:T(1024)} %get-tuple-element.44) | copy-start | bytes 24580
  (78 other events, 781.5 us)
Sparse Core Ops, SparseCore 0:
  10.8 40.5 all-gather.9
  54.2 37.6 all-gather.11
  94.7 51.2 all-gather.13
  148.6 48.8 all-gather.15
  204.6 62.0 all-reduce.8
  269.3 126.4 all-gather.19
  398.6 124.5 all-gather.17
  526.0 124.5 all-gather.21
  702.6 61.1 all-reduce.10
  811.9 21.8 reduce-scatter.13
  855.8 21.7 reduce-scatter.11
  881.1 55.9 reduce-scatter.19
  941.2 56.6 reduce-scatter.17
  1000.9 106.9 all-reduce.12
  1111.6 72.9 reduce-scatter.21
  1188.3 71.8 reduce-scatter.15
  1264.2 176.4 reduce-scatter.27
  1444.6 176.4 reduce-scatter.25
  1625.2 176.4 reduce-scatter.23
where the time goes:
time: 1820 us; the launch traced here: 1810 us
  waiting for transfers between devices  1200 us (66%)
  matrix products  270 us (15%)
  blocking collectives  162 us (9%)
  other arithmetic  112 us (6%)
  local copies, waits for them, and re-layouts  44.3 us (2%)
    reduce_scatter x6, waiting for transfers between devices, summed(): lax.psum_scatter(term.astype(jnp.bfloat16), ('dp', 'seq'), scatter_dimens...  450 us
    all_gather x3, waiting for transfers between devices, local(): lax.all_gather(for_sending(mlp_pack()), ('dp', 'seq'), axis=0, tiled=True)  349 us
    unnamed x20, waiting for transfers between devices  179 us
    psum x1, waiting for transfers between devices, local(): lax.psum(times_transposed(hidden, mlp_set[3]).astype(jnp.bfloat16), 'tens...  108 us
    dot_general x7, matrix products, transposed_times(): lax.dot_general(left_side, right_side, (((0,), (0,)), ((), ())), preferre...  63.4 us
    unnamed x1, blocking collectives  62.4 us
    dot_general x7, matrix products, times_transposed(): lax.dot_general(left_side, right_side, (((1,), (1,)), ((), ())), preferre...  56.9 us
    all_gather x4, waiting for transfers between devices, local(): lax.all_gather(for_sending(attn_pack()), ('dp', 'seq'), axis=0, tiled=True)  47.7 us
  transfers between devices with their start and end apart: 19, of which 15 were waited for; matrix products, arithmetic and copies ran while one was open for 17% of the time, Pallas kernels for 0%

commit v1 on v0

--- a/solution.py
+++ b/solution.py
@@ -82,6 +82,11 @@
     up_weight,
     down_weight,
 ):
+
+    def resolve_cycles(patch):
+        item_now = lax.all_gather(patch, axis_name="tensor").sum(axis=0)
+        return item_now
+
     seq_count = lax.axis_size("seq")
     seq_rank = lax.axis_index("seq")
     tok_rows = tokens.shape[0]
@@ -202,11 +207,10 @@
         grad_hidden * upward * sigmoid_gate * (1.0 + gate_pre * (1.0 - sigmoid_gate))
     ).astype(jnp.bfloat16)
     grad_up = (grad_hidden * activated).astype(jnp.bfloat16)
-    grad_normed_two = lax.psum(
+    grad_normed_two = resolve_cycles(
         (times_transposed(grad_gate, mlp_set[1]) + times_transposed(grad_up, mlp_set[2])).astype(
             jnp.bfloat16
-        ),
-        "tensor",
+        )
     ).astype(jnp.float32)
     gain_two_grad = jnp.sum(grad_normed_two * unit_two, axis=0)
     grad_middle = grad_out + norm_back(

time: 1820 us -> 1820 us (level)
    psum x1 -> x0, waiting for transfers between devices: 45.5 us -> none  [local(): lax.psum((times_transposed(grad_gate, mlp_set[1]) + times_transposed(grad...]
    all_gather x0 -> x1, waiting for transfers between devices: none -> 39.4 us  [resolve_cycles(): item_now = lax.all_gather(patch, axis_name='tensor').sum(axis=0)]
    unnamed x175 -> x183, local copies, waits for them, and re-layouts: 37.5 us -> 37.6 us
where the time goes in v1:
time: 1820 us; the launch traced here: 1810 us
  waiting for transfers between devices  1200 us (66%)
  matrix products  270 us (15%)
  blocking collectives  162 us (9%)
  other arithmetic  115 us (6%)
  local copies, waits for them, and re-layouts  44.4 us (2%)
    reduce_scatter x6, waiting for transfers between devices, summed(): lax.psum_scatter(term.astype(jnp.bfloat16), ('dp', 'seq'), scatter_dimens...  450 us
    all_gather x3, waiting for transfers between devices, local(): lax.all_gather(for_sending(mlp_pack()), ('dp', 'seq'), axis=0, tiled=True)  349 us
    unnamed x20, waiting for transfers between devices  179 us
    psum x1, waiting for transfers between devices, local(): lax.psum(times_transposed(hidden, mlp_set[3]).astype(jnp.bfloat16), 'tens...  109 us
    dot_general x7, matrix products, transposed_times(): lax.dot_general(left_side, right_side, (((0,), (0,)), ((), ())), preferre...  63.4 us
    unnamed x1, blocking collectives  62.4 us
    dot_general x7, matrix products, times_transposed(): lax.dot_general(left_side, right_side, (((1,), (1,)), ((), ())), preferre...  56.6 us
    all_gather x4, waiting for transfers between devices, local(): lax.all_gather(for_sending(attn_pack()), ('dp', 'seq'), axis=0, tiled=True)  47.7 us
  transfers between devices with their start and end apart: 19, of which 15 were waited for; matrix products, arithmetic and copies ran while one was open for 17% of the time, Pallas kernels for 0%

profile of v1, /device:TPU:0, one launch (start us, length us, event | category | flops | bytes accessed | tf_op | source)
XLA Modules:
  0.0 1810.0 jit_solution(14175947568555046593)
XLA Ops:
  18.5 33.9 %all-gather.1 = bf16[16,1,128]{2,1,0:T(2,128)(2,1)S(1)} all-gather(bf16[1,1,128]{2,1,0:T(2,128)(2,1)S(1)} %convert_bitcast_fusion.2), channel_id=1, replica_groups=mesh['dp'=4,'seq'=4,'tensor'=2] {'dp','seq'}, dimensions={0}, use_global_device_ids=true | all-gather | bytes 4352 | tf_op jit(solution)/shard_map/all_gather | solution.py:133
  57.3 15.7 all_gather.41
  76.1 15.8 all-gather.14.cloned.1.call-done
  94.3 19.1 %all_gather.43 = bf16[1024,256]{0,1:T(8,128)(2,1)S(1)} all-gather(bf16[256,256]{0,1:T(8,128)(2,1)S(1)} %bitcast.281), channel_id=1, replica_groups=mesh['dp'=4,'seq'=4,'tensor'=2] {'seq'}, dimensions={0}, use_global_device_ids=true | all-gather | bytes 655360 | tf_op jit(solution)/shard_map/all_gather | solution.py:154
  114.1 31.9 %all-gather.16.cloned.1.call-done = bf16[2048,1024]{1,0:T(8,128)(2,1)} async-done(((bf16[128,1024]{1,0:T(8,128)(2,1)}), bf16[2048,1024]{1,0:T(8,128)(2,1)}) %all-gather.16.cloned.1.call-update) | async-done | bytes 4194320 | tf_op jit(solution)/shard_map/all_gather | solution.py:133
  212.9 31.3 %all-gather.2 = bf16[16,1,128]{2,1,0:T(2,128)(2,1)S(1)} all-gather(bf16[1,1,128]{2,1,0:T(2,128)(2,1)S(1)} %convert_bitcast_fusion.1), channel_id=1, replica_groups=mesh['dp'=4,'seq'=4,'tensor'=2] {'dp','seq'}, dimensions={0}, use_global_device_ids=true | all-gather | bytes 4352 | tf_op jit(solution)/shard_map/all_gather | solution.py:134
  244.2 22.5 %all-reduce.8.cloned.1.call-done = bf16[512,2048]{1,0:T(8,128)(2,1)} async-done(((bf16[512,2048]{1,0:T(8,128)(2,1)}), bf16[512,2048]{1,0:T(8,128)(2,1)}) %all-reduce.8.cloned.1.call-update) | async-done | bytes 2097168 | tf_op jit(solution)/shard_map/psum | solution.py:190
  271.6 124.2 %all-gather.22.cloned.1.call-done = bf16[2048,4096]{1,0:T(8,128)(2,1)} async-done(((bf16[128,4096]{1,0:T(8,128)(2,1)}), bf16[2048,4096]{1,0:T(8,128)(2,1)}) %all-gather.22.cloned.1.call-update) | async-done | bytes 16777232 | tf_op jit(solution)/shard_map/all_gather | solution.py:134
  395.8 15.1 fusion.159
  411.0 112.3 %all-gather.20.cloned.1.call-done = bf16[2048,4096]{1,0:T(8,128)(2,1)} async-done(((bf16[128,4096]{1,0:T(8,128)(2,1)}), bf16[2048,4096]{1,0:T(8,128)(2,1)}) %all-gather.20.cloned.1.call-update) | async-done | bytes 16777232 | tf_op jit(solution)/shard_map/all_gather | solution.py:134
  523.3 15.0 fusion.158
  538.3 112.4 %all-gather.24.cloned.1.call-done = bf16[2048,4096]{1,0:T(8,128)(2,1)} async-done(((bf16[128,4096]{1,0:T(8,128)(2,1)}), bf16[2048,4096]{1,0:T(8,128)(2,1)}) %all-gather.24.cloned.1.call-update) | async-done | bytes 16777232 | tf_op jit(solution)/shard_map/all_gather | solution.py:134
  650.7 22.2 %multiply_convert_fusion = (bf16[512,4096]{1,0:T(8,128)(2,1)}, bf16[512,4096]{1,0:T(8,128)(2,1)}, bf16[512,4096]{1,0:T(8,128)(2,1)}) fusion(f32[512,4096]{1,0:T(8,128)} %fusion.158, f32[512,4096]{1,0:T(8,128)} %fusion.159, bf16[512,2048]{1,0:T(8,128)(2,1)} %param.14, bf16[2048,4096]{1,0:T(8,128)(2,1)} %all-gather.24.cloned.1.call-done), kind=kOutput, calls=%fused_computation.43 | convolution fusion | flops 8621391872 | bytes 48234496 | tf_op jit(solution)/shard_map/dot_general | solution.py:205
  672.8 15.4 fusion.160
  702.7 15.5 convolution_convert_fusion.5
  718.2 39.4 %all-gather.26.cloned.1.call-done = bf16[1024,2048]{1,0:T(8,128)(2,1)} async-done(((bf16[512,2048]{1,0:T(8,128)(2,1)}), bf16[1024,2048]{1,0:T(8,128)(2,1)}) %all-gather.26.cloned.1.call-update) | async-done | bytes 4194320 | tf_op jit(solution)/shard_map/all_gather | solution.py:87
  922.6 21.0 %copy.109 = bf16[2048,4096]{1,0:T(8,128)(2,1)} copy(bf16[2048,4096]{0,1:T(8,128)(2,1)} %convert_bitcast_fusion) | data formatting | bytes 33554432
  977.4 18.7 %reduce-scatter.18.cloned.1.call-done = bf16[128,256]{1,0:T(8,128)(2,1)} async-done(((bf16[2048,256]{1,0:T(8,128)(2,1)}), bf16[128,256]{1,0:T(8,128)(2,1)}) %reduce-scatter.18.cloned.1.call-update) | async-done | bytes 65552 | tf_op jit(solution)/shard_map/reduce_scatter | solution.py:221
  997.7 108.9 %all-reduce.10.cloned.1.call-done = (bf16[512,2048]{1,0:T(8,128)(2,1)}, bf16[512,2048]{1,0:T(8,128)(2,1)}) async-done(((bf16[512,2048]{1,0:T(8,128)(2,1)}, bf16[512,2048]{1,0:T(8,128)(2,1)}), (bf16[512,2048]{1,0:T(8,128)(2,1)}, bf16[512,2048]{1,0:T(8,128)(2,1)})) %all-reduce.10.cloned.1.call-update) | async-done | bytes 4194320 | tf_op jit(solution)/shard_map/psum | solution.py:200
  1109.5 62.4 %all-reduce.3 = (f32[2048]{0:T(1024)S(1)}, f32[2048]{0:T(1024)S(1)}) all-reduce(f32[2048]{0:T(1024)S(1)} %get-tuple-element.46, f32[2048]{0:T(1024)S(1)} %copy-done.58), channel_id=5, replica_groups=mesh['dp'=4,'seq'=4,'tensor'=2] {'dp','seq'}, use_global_device_ids=true, to_apply=%region_23.24.clone | all-reduce | flops 4096 | bytes 32768
  1185.1 73.9 %reduce-scatter.16.cloned.1.call-done = bf16[128,1024]{1,0:T(8,128)(2,1)} async-done(((bf16[2048,1024]{1,0:T(8,128)(2,1)}), bf16[128,1024]{1,0:T(8,128)(2,1)}) %reduce-scatter.16.cloned.1.call-update) | async-done | bytes 262160 | tf_op jit(solution)/shard_map/reduce_scatter | solution.py:221
  1260.8 178.6 %reduce-scatter.28.cloned.1.call-done = bf16[128,4096]{1,0:T(8,128)(2,1)} async-done(((bf16[2048,4096]{1,0:T(8,128)(2,1)}), bf16[128,4096]{1,0:T(8,128)(2,1)}) %reduce-scatter.28.cloned.1.call-update) | async-done | bytes 1048592
  1442.7 177.2 %reduce-scatter.26.cloned.1.call-done = bf16[128,4096]{1,0:T(8,128)(2,1)} async-done(((bf16[2048,4096]{1,0:T(8,128)(2,1)}), bf16[128,4096]{1,0:T(8,128)(2,1)}) %reduce-scatter.26.cloned.1.call-update) | async-done | bytes 1048592 | tf_op jit(solution)/shard_map/reduce_scatter | solution.py:221
  1622.6 177.8 %reduce-scatter.24.cloned.1.call-done = bf16[128,4096]{1,0:T(8,128)(2,1)} async-done(((bf16[2048,4096]{1,0:T(8,128)(2,1)}), bf16[128,4096]{1,0:T(8,128)(2,1)}) %reduce-scatter.24.cloned.1.call-update) | async-done | bytes 1048592 | tf_op jit(solution)/shard_map/reduce_scatter | solution.py:221
  (350 shorter events, 333.5 us)
Async XLA Ops:
  7.2 48.1 %all-gather.12.cloned.1.call-start = ((), (), s32[]{:S(2)}) async-start(), calls=%async_computation.9 | async-start | bytes 1114112 | tf_op jit(solution)/shard_map/all_gather | solution.py:133
  9.0 82.9 %all-gather.14.cloned.1.call-start = ((), (), s32[]{:S(2)}) async-start(), calls=%async_computation.10 | async-start | bytes 1114112 | tf_op jit(solution)/shard_map/all_gather | solution.py:133
  10.6 135.3 %all-gather.16.cloned.1.call-start = ((), (), s32[]{:S(2)}) async-start(), calls=%async_computation.11 | async-start | bytes 4456448 | tf_op jit(solution)/shard_map/all_gather | solution.py:133
  12.4 185.8 %all-gather.18.cloned.1.call-start = ((), (), s32[]{:S(2)}) async-start(), calls=%async_computation.12 | async-start | bytes 4456448 | tf_op jit(solution)/shard_map/all_gather | solution.py:133
  14.3 252.4 %all-reduce.8.cloned.1.call-start = ((), (), s32[]{:S(2)}) async-start(), calls=%async_computation.13 | async-start | bytes 4194304 | tf_op jit(solution)/shard_map/psum | solution.py:190
  18.5 127.4 %copy-start.59 = (f32[512]{0:T(512)}, f32[512]{0:T(512)S(1)}, u32[]{:S(2)}) copy-start(f32[512]{0:T(512)S(1)} %add_rsqrt_fusion.1) | copy-start | bytes 6148
  52.4 93.5 %copy-start.50 = (f32[16,1,128]{2,1,0:T(1,128)}, f32[16,1,128]{2,1,0:T(1,128)S(1)}, u32[]{:S(2)}) copy-start(f32[16,1,128]{2,1,0:T(1,128)S(1)} %convert_element_type.285) | copy-start | bytes 24580
  54.0 96.8 %copy-start.16 = (f32[512,64]{0,1:T(8,128)}, f32[512,64]{0,1:T(8,128)S(1)}, u32[]{:S(2)}) copy-start(f32[512,64]{0,1:T(8,128)S(1)} %get-tuple-element.70) | copy-start | bytes 393220
  94.3 73.3 %copy-start.11 = (bf16[256,4,64]{0,2,1:T(8,128)(2,1)}, bf16[256,4,64]{0,2,1:T(8,128)(2,1)S(1)}, u32[]{:S(2)}) copy-start(bf16[256,4,64]{0,2,1:T(8,128)(2,1)S(1)} %get-tuple-element.68) | copy-start | bytes 393220
  204.5 191.3 %all-gather.22.cloned.1.call-start = ((), (), s32[]{:S(2)}) async-start(), calls=%async_computation.15 | async-start | bytes 17825792 | tf_op jit(solution)/shard_map/all_gather | solution.py:134
  207.3 315.9 %all-gather.20.cloned.1.call-start = ((), (), s32[]{:S(2)}) async-start(), calls=%async_computation.14 | async-start | bytes 17825792 | tf_op jit(solution)/shard_map/all_gather | solution.py:134
  210.1 440.6 %all-gather.24.cloned.1.call-start = ((), (), s32[]{:S(2)}) async-start(), calls=%async_computation.16 | async-start | bytes 17825792 | tf_op jit(solution)/shard_map/all_gather | solution.py:134
  212.8 544.7 %all-gather.26.cloned.1.call-start = ((), (), s32[]{:S(2)}) async-start(), calls=%async_computation.25 | async-start | bytes 6291456 | tf_op jit(solution)/shard_map/all_gather | solution.py:87
  702.5 160.7 %reduce-scatter.14.cloned.1.call-start = ((), (), s32[]{:S(2)}) async-start(), calls=%async_computation.18 | async-start | bytes 655360 | tf_op jit(solution)/shard_map/reduce_scatter | solution.py:271
  810.5 65.9 %reduce-scatter.12.cloned.1.call-start = ((), (), s32[]{:S(2)}) async-start(), calls=%async_computation.17 | async-start | bytes 655360 | tf_op jit(solution)/shard_map/reduce_scatter | solution.py:268
  854.5 121.5 %reduce-scatter.20.cloned.1.call-start = ((), (), s32[]{:S(2)}) async-start(), calls=%async_computation.21 | async-start | bytes 1114112 | tf_op jit(solution)/shard_map/reduce_scatter | solution.py:221
  866.4 129.8 %reduce-scatter.18.cloned.1.call-start = ((), (), s32[]{:S(2)}) async-start(), calls=%async_computation.20 | async-start | bytes 1114112 | tf_op jit(solution)/shard_map/reduce_scatter | solution.py:221
  882.2 224.4 %all-reduce.10.cloned.1.call-start = ((), (), s32[]{:S(2)}) async-start(), calls=%async_computation.27 | async-start | bytes 8388608 | tf_op jit(solution)/shard_map/psum | solution.py:200
  891.7 291.6 %reduce-scatter.22.cloned.1.call-start = ((), (), s32[]{:S(2)}) async-start(), calls=%async_computation.22 | async-start | bytes 4456448 | tf_op jit(solution)/shard_map/reduce_scatter | solution.py:221
  901.7 357.2 %reduce-scatter.16.cloned.1.call-start = ((), (), s32[]{:S(2)}) async-start(), calls=%async_computation.19 | async-start | bytes 4456448 | tf_op jit(solution)/shard_map/reduce_scatter | solution.py:221
  907.6 531.9 %reduce-scatter.28.cloned.1.call-start = ((), (), s32[]{:S(2)}) async-start(), calls=%async_computation.26 | async-start | bytes 17825792
  943.6 676.2 %reduce-scatter.26.cloned.1.call-start = ((), (), s32[]{:S(2)}) async-start(), calls=%async_computation.24 | async-start | bytes 17825792 | tf_op jit(solution)/shard_map/reduce_scatter | solution.py:221
  958.7 841.7 %reduce-scatter.24.cloned.1.call-start = ((), (), s32[]{:S(2)}) async-start(), calls=%async_computation.23 | async-start | bytes 17825792 | tf_op jit(solution)/shard_map/reduce_scatter | solution.py:221
  974.0 135.5 %copy-start.58 = (f32[2048]{0:T(1024)S(1)}, f32[2048]{0:T(1024)}, u32[]{:S(2)}) copy-start(f32[2048]{0:T(1024)} %get-tuple-element.44) | copy-start | bytes 24580
  (82 other events, 886.4 us)
Sparse Core Ops, SparseCore 0:
  10.8 40.5 all-gather.11
  54.2 37.6 all-gather.13
  94.7 51.2 all-gather.15
  148.6 48.9 all-gather.17
  204.7 62.0 all-reduce.7
  269.4 126.4 all-gather.21
  398.6 124.5 all-gather.19
  526.0 124.5 all-gather.23
  702.7 54.8 all-gather.25
  810.7 21.8 reduce-scatter.13
  854.6 21.8 reduce-scatter.11
  879.9 55.9 reduce-scatter.19
  939.5 56.6 reduce-scatter.17
  999.7 106.8 all-reduce.9
  1110.3 72.9 reduce-scatter.21
  1187.0 71.8 reduce-scatter.15
  1262.9 176.4 reduce-scatter.27
  1443.4 176.4 reduce-scatter.25
  1624.0 176.4 reduce-scatter.23
